TPU v7x, 32 devices: a whole 2x2x4 slice. The times are simulated.
32 devices in a mesh: scene: 4 (over x, core), frame: 8 (over z, y).
Axes of the slice: x: 2, y: 2, z: 4, core: 2. Of those that a mesh axis runs over, the one named last changes fastest.
Arguments:
- features: bfloat16 [8192, 1024], P(('scene', 'frame')), parts along dimension 0, may hold values from -1.5 to 1.5
- norm_gain: float32 [1024], replicated, may hold values from 0.1 to 1.9
- w_qkv: bfloat16 [1024, 3072], replicated, may hold values from -1.3125 to 1.3125
- w_out: bfloat16 [1024, 1024], replicated, may hold values from -0.1875 to 0.1875
- counts: int32 [32], P('scene'), parts along dimension 0, may hold values from 1 to 32, as said below
- query_index: int32 [32, 32], P(('scene', 'frame')), parts along dimension 0, may hold values from 0 to 255
- owner: int32 [32], P('scene'), parts along dimension 0, may hold values from 0 to 7
Outputs:
- mixed: bfloat16 [8192, 1024], P(('scene', 'frame')), parts along dimension 0
- correlation: float32 [32, 8, 32, 256], P(('scene', 'frame')), parts along dimension 0
There are 4 independent parts, one for each index of `scene`. A program takes and returns all parts, laid end to end along the dimension named above; an argument that names none is the same for every part. Nothing has to cross between parts.
Inputs may be any that keep to these rules, and one draw needn't show every extreme that they name: `counts`: every frame has at least one query and some frame has exactly 32.
All inputs are finite; a program needn't handle non-finite values.
Results may differ from a plain program's by a relative error of at most 0.017.
The roundings to bfloat16 on the way count: a program that leaves them out, or rounds other values in their place, can miss the bound.
Values may be sent and summed in bfloat16 or wider, within the bound.
A program may use at most 256 MiB of HBM per device.

v0:
```python
import jax
import jax.numpy as jnp
from jax import lax
from jax.sharding import PartitionSpec as P

D = 1024
HEADS = 16


def normalize(x, gain):
    xf = x.astype(jnp.float32)
    mean = jnp.mean(xf, axis=-1, keepdims=True)
    var = jnp.mean((xf - mean) ** 2, axis=-1, keepdims=True)
    return ((xf - mean) * lax.rsqrt(var + 1e-05) * gain).astype(jnp.bfloat16)


def per_device(features, norm_gain, w_qkv, w_out, counts, query_index, owner):
    tok = features.shape[0]
    head_dim = D // HEADS
    normed = normalize(features, norm_gain)
    proj = jnp.dot(normed, w_qkv, preferred_element_type=jnp.float32)
    queries = (
        (proj[:, :D] * (1.0 / head_dim**0.5)).astype(jnp.bfloat16).reshape(tok, HEADS, head_dim)
    )
    keys = proj[:, D : 2 * D].astype(jnp.bfloat16)
    values = proj[:, 2 * D :].astype(jnp.bfloat16)
    top = jnp.full((HEADS, tok), -1e30, jnp.float32)
    kpart = lax.all_gather(keys, "frame", axis=0, tiled=True)
    vpart = lax.all_gather(values, "frame", axis=0, tiled=True)
    count = kpart.shape[0]
    scores = jnp.einsum(
        "thd,shd->hts",
        queries,
        kpart.reshape(count, HEADS, head_dim),
        preferred_element_type=jnp.float32,
    )
    newtop = jnp.maximum(top, jnp.max(scores, axis=-1))
    weights = jnp.exp(scores - newtop[:, :, None])
    total = jnp.sum(weights, axis=-1)
    accum = jnp.einsum(
        "hts,shd->htd",
        weights.astype(jnp.bfloat16),
        vpart.reshape(count, HEADS, head_dim),
        preferred_element_type=jnp.float32,
    )
    top, total, accum = (newtop, total, accum)
    attended = (
        jnp.transpose(accum / total[:, :, None], (1, 0, 2)).reshape(tok, D).astype(jnp.bfloat16)
    )
    mixed = (
        features.astype(jnp.float32) + jnp.dot(attended, w_out, preferred_element_type=jnp.float32)
    ).astype(jnp.bfloat16)
    mine = lax.axis_index("frame")
    slots = query_index[0]
    picked = mixed[slots]
    valid = jnp.arange(slots.shape[0]) < counts[mine]
    picked = jnp.where(valid[:, None], picked, jnp.zeros_like(picked))
    arrived = lax.all_gather(picked[None], "frame", axis=0, tiled=True)
    corr = jnp.einsum("fqd,td->fqt", arrived, mixed, preferred_element_type=jnp.float32) * (
        1.0 / D**0.5
    )
    owned = owner == mine
    corr = jnp.where(owned[:, None, None], corr, jnp.float32(0.0))
    return (mixed, corr[None])


def solution(mesh):
    in_specs = (
        P(("scene", "frame"), None),
        P(),
        P(),
        P(),
        P("scene"),
        P(("scene", "frame"), None),
        P("scene"),
    )
    out_specs = (P(("scene", "frame"), None), P(("scene", "frame"), None, None, None))
    return jax.shard_map(
        per_device, mesh=mesh, in_specs=in_specs, out_specs=out_specs, check_vma=False
    )
```

profile of v0, /device:TPU:0, one launch (start us, length us, event | category | flops | bytes accessed | tf_op | source)
XLA Modules:
  0.0 230.9 jit_solution(3994920506731051241)
XLA Ops:
  7.2 0.0 copy-start
  7.2 0.0 all-gather.3.cloned.1.call-start
  7.2 1.3 convert_reduce_fusion
  8.6 1.3 fusion.13
  9.9 6.6 %fusion.27 = (bf16[256,3072]{1,0:T(8,128)(2,1)S(1)}, f32[256,3072]{1,0:T(8,128)}) fusion(bf16[1024,3072]{1,0:T(8,128)(2,1)} %param.9, bf16[256,1024]{1,0:T(8,128)(2,1)} %param.7, f32[1024]{0:T(1024)} %param.8, f32[256]{0:T(256)S(1)} %add_rsqrt_fusion, f32[256]{0:T(256)S(1)} %broadcast_multiply_fusion), kind=kOutput, calls=%fused_computation.37 | convolution fusion | flops 1612709888 | bytes 11540480 | tf_op jit(solution)/shard_map/dot_general | solution.py:21
  16.5 0.0 copy-start.3
  16.5 0.0 copy-start.4
  16.5 0.0 copy-start.5
  16.5 1.0 fusion.26
  17.5 0.0 all-gather.3.cloned.1.call-update
  17.5 0.0 all-gather.5.cloned.1.call-start
  17.6 0.7 all-gather.5.cloned.1.call-update
  18.3 1.3 fusion.16
  19.6 0.2 copy.15
  19.8 0.0 copy-done.3
  19.8 0.6 dynamic_slice.3
  20.4 0.6 iota_compare_fusion
  21.1 0.0 copy-done.4
  21.1 0.0 copy-done.5
  21.1 72.1 %all-gather.3.cloned.1.call-done = bf16[2048,1024]{1,0:T(8,128)(2,1)} async-done(((bf16[256,1024]{1,0:T(8,128)(2,1)}), bf16[2048,1024]{1,0:T(8,128)(2,1)}) %all-gather.3.cloned.1.call-update) | async-done | bytes 4194320 | tf_op jit(solution)/shard_map/all_gather | solution.py:28
  93.2 6.5 %copy.16 = bf16[2048,1024]{0,1:T(8,128)(2,1)} copy(bf16[2048,1024]{1,0:T(8,128)(2,1)} %all-gather.3.cloned.1.call-done) | data formatting | bytes 8388608 | tf_op jit(solution)/shard_map/all_gather | solution.py:28
  99.7 15.8 %fusion.28 = (f32[16,256]{1,0:T(8,128)S(1)}, f32[16,256,2048]{2,1,0:T(8,128)}) fusion(bf16[256,16,64]{0,2,1:T(8,128)(2,1)S(1)} %bitcast.30, bf16[2048,16,64]{0,2,1:T(8,128)(2,1)} %bitcast.28), kind=kOutput, calls=%fused_computation.38 | convolution fusion | flops 1082126336 | bytes 38289408 | tf_op jit(solution)/shard_map/thd,shd->hts/dot_general | solution.py:31
  115.5 14.0 %fusion = f32[16,256]{1,0:T(8,128)S(1)} fusion(f32[16,256,2048]{2,1,0:T(8,128)} %get-tuple-element.7, f32[16,256]{1,0:T(8,128)S(1)} %broadcast_maximum_fusion), kind=kLoop, calls=%fused_computation.2 | loop fusion | flops 16773120 | bytes 33587200 | tf_op jit(solution)/shard_map/reduce_sum | solution.py:39
  129.5 37.2 %all-gather.5.cloned.1.call-done = bf16[2048,1024]{1,0:T(8,128)(2,1)} async-done(((bf16[256,1024]{1,0:T(8,128)(2,1)}), bf16[2048,1024]{1,0:T(8,128)(2,1)}) %all-gather.5.cloned.1.call-update) | async-done | bytes 4194320 | tf_op jit(solution)/shard_map/all_gather | solution.py:29
  166.7 6.5 %copy.17 = bf16[2048,1024]{0,1:T(8,128)(2,1)} copy(bf16[2048,1024]{1,0:T(8,128)(2,1)} %all-gather.5.cloned.1.call-done) | data formatting | bytes 8388608 | tf_op jit(solution)/shard_map/all_gather | solution.py:29
  173.2 0.0 copy-start.2
  173.2 15.7 %divide_convert_fusion = bf16[256,16,64]{0,2,1:T(8,128)(2,1)} fusion(bf16[2048,16,64]{0,2,1:T(8,128)(2,1)} %bitcast.29, f32[16,256,2048]{2,1,0:T(8,128)} %get-tuple-element.7, f32[16,256]{1,0:T(8,128)S(1)} %broadcast_maximum_fusion, f32[256,16]{0,1:T(8,128)S(1)} %bitcast.32), kind=kOutput, calls=%fused_computation.21 | convolution fusion | flops 1091043328 | bytes 38305792 | tf_op jit(solution)/shard_map/hts,shd->htd/dot_general | solution.py:40
  188.9 0.0 copy-done
  188.9 0.0 copy-done.2
  188.9 1.8 fusion.8
  190.7 0.0 copy-start.1
  190.7 0.6 gather_fusion
  191.3 0.1 bitcast_select_fusion
  191.4 31.6 %all_gather.11 = bf16[8,32,1024]{2,1,0:T(8,128)(2,1)S(1)} all-gather(bf16[1,32,1024]{2,1,0:T(8,128)(2,1)S(1)} %bitcast_select_fusion), channel_id=1, replica_groups=mesh['scene'=4,'frame'=8] {'frame'}, dimensions={0}, use_global_device_ids=true | all-gather | bytes 589824 | tf_op jit(solution)/shard_map/all_gather | solution.py:58
  223.0 1.1 fusion.12
  224.0 0.0 copy-done.1
  (6 shorter events, 0.0 us)
Async XLA Ops:
  7.2 181.7 %copy-start = (bf16[1024,1024]{1,0:T(8,128)(2,1)S(1)}, bf16[1024,1024]{1,0:T(8,128)(2,1)}, u32[]{:S(2)}) copy-start(bf16[1024,1024]{1,0:T(8,128)(2,1)} %param.10) | copy-start | bytes 6291460
  7.2 86.0 %all-gather.3.cloned.1.call-start = ((), (), s32[]{:S(2)}) async-start(), calls=%async_computation | async-start | bytes 4718592 | tf_op jit(solution)/shard_map/all_gather | solution.py:28
  16.5 3.4 %copy-start.3 = (s32[8]{0:T(128)S(1)}, s32[8]{0:T(128)}, u32[]{:S(2)}) copy-start(s32[8]{0:T(128)} %param.11) | copy-start | bytes 100
  16.5 4.6 %copy-start.4 = (s32[1,32]{1,0:T(1,128)S(1)}, s32[1,32]{1,0:T(1,128)}, u32[]{:S(2)}) copy-start(s32[1,32]{1,0:T(1,128)} %param.12) | copy-start | bytes 388
  16.5 4.7 %copy-start.5 = (s32[8]{0:T(128)S(1)}, s32[8]{0:T(128)}, u32[]{:S(2)}) copy-start(s32[8]{0:T(128)} %param.13) | copy-start | bytes 100
  17.5 149.2 %all-gather.5.cloned.1.call-start = ((), (), s32[]{:S(2)}) async-start(), calls=%async_computation.1 | async-start | bytes 4718592 | tf_op jit(solution)/shard_map/all_gather | solution.py:29
  173.2 15.7 %copy-start.2 = (bf16[256,1024]{1,0:T(8,128)(2,1)S(1)}, bf16[256,1024]{1,0:T(8,128)(2,1)}, u32[]{:S(2)}) copy-start(bf16[256,1024]{1,0:T(8,128)(2,1)} %param.7) | copy-start | bytes 1572868
  190.7 33.3 %copy-start.1 = (bf16[256,1024]{1,0:T(8,128)(2,1)}, bf16[256,1024]{1,0:T(8,128)(2,1)S(1)}, u32[]{:S(2)}) copy-start(bf16[256,1024]{1,0:T(8,128)(2,1)S(1)} %fusion.8) | copy-start | bytes 1572868
Sparse Core Ops, SparseCore 0:
  17.7 75.5 all-gather.2
  95.3 71.3 all-gather.4
where the time goes:
time: 232 us; the launch traced here: 231 us
  waiting for transfers between devices  110 us (47%)
  matrix products  40.9 us (18%)
  blocking collectives  31.6 us (14%)
  other arithmetic  18.7 us (8%)
  local copies, waits for them, and re-layouts  15.5 us (7%)
  between operations  14.2 us (6%)
    all_gather x1, waiting for transfers between devices, per_device(): kpart = lax.all_gather(keys, 'frame', axis=0, tiled=True)  72.1 us
    all_gather x1, waiting for transfers between devices, per_device(): vpart = lax.all_gather(values, 'frame', axis=0, tiled=True)  37.2 us
    all_gather x1, blocking collectives, per_device(): arrived = lax.all_gather(picked[None], 'frame', axis=0, tiled=True)  31.6 us
    dot_general x1, matrix products, per_device(): jnp.einsum('thd,shd->hts', queries, kpart.reshape(count, HEADS, head_dim)...  15.8 us
    dot_general x1, matrix products, per_device(): jnp.einsum('hts,shd->htd', weights.astype(jnp.bfloat16), vpart.reshape(co...  15.7 us
    reduce_sum x1, other arithmetic, per_device(): total = jnp.sum(weights, axis=-1)  14 us
    dot_general x1, matrix products, per_device(): proj = jnp.dot(normed, w_qkv, preferred_element_type=jnp.float32)  6.56 us
    all_gather x1, local copies, waits for them, and re-layouts, per_device(): kpart = lax.all_gather(keys, 'frame', axis=0, tiled=True)  6.5 us
  transfers between devices with their start and end apart: 2, of which 2 were waited for; matrix products, arithmetic and copies ran while one was open for 17% of the time, Pallas kernels for 0%

commit v1 on v0

v1 whole, which is shorter than its diff:
```python
import functools

import jax
import jax.numpy as jnp
from jax import lax
from jax.experimental import pallas as pl
from jax.experimental.pallas import tpu as pltpu
from jax.sharding import PartitionSpec as P

HEADS = 16
MESH = pl.DeviceIdType.MESH
F32 = jnp.float32
BF16 = jnp.bfloat16
NT = (((1,), (1,)), ((), ()))
GROUP = 4


def kernel(
    n,
    f_ref, gain_ref, wqkv_hbm, wo_hbm, counts_ref, index_ref, owner_ref,
    mixed_ref, corr_ref,
    slots, w, wo, wvt, nrm, qt, kb, vt, acc, top, total, rows,
    wsem, send, recv, rsend, rrecv,
):
    tok, d = f_ref.shape
    hd = d // HEADS
    length = n // 2
    me = lax.axis_index("frame")
    a, b = me // 2, me % 2
    across = a * 2 + (1 - b)
    has_left, has_right = a > 0, a < length - 1

    copies = [
        pltpu.make_async_copy(wqkv_hbm, w, wsem.at[0]),
        pltpu.make_async_copy(wo_hbm, wo, wsem.at[1]),
    ]
    for c in copies:
        c.start()

    barrier = pltpu.get_barrier_semaphore()

    def greet(target):
        pl.semaphore_signal(barrier, inc=1, device_id={"frame": target}, device_id_type=MESH)

    pl.when(has_left)(lambda: greet(me - 2))
    pl.when(has_right)(lambda: greet(me + 2))
    greet(across)
    pl.semaphore_wait(
        barrier, 1 + jnp.where(has_left, 1, 0) + jnp.where(has_right, 1, 0)
    )

    def hop(buf, ssem, rsem, src, way, target, source=None):
        return pltpu.make_async_remote_copy(
            src_ref=buf.at[src] if source is None else source,
            dst_ref=buf.at[src],
            send_sem=ssem.at[src // 2, way],
            recv_sem=rsem.at[src],
            device_id={"frame": target},
            device_id_type=MESH,
        )

    def push(buf, ssem, rsem, src, go_right, go_left, source=None):
        pl.when(go_right)(lambda: hop(buf, ssem, rsem, src, 0, me + 2, source).start())
        pl.when(go_left)(lambda: hop(buf, ssem, rsem, src, 1, me - 2, source).start())
        hop(buf, ssem, rsem, src, 2, across, source).start()

    def landed(buf, ssem, rsem, src):
        hop(buf, ssem, rsem, src, 2, across).wait_recv()

    def relay(buf, ssem, rsem, dist):
        @pl.when(a - dist >= 0)
        def _():
            src = me - 2 * dist
            landed(buf, ssem, rsem, src)
            push(buf, ssem, rsem, src, has_right, False)

        @pl.when(a + dist <= length - 1)
        def _():
            src = me + 2 * dist
            landed(buf, ssem, rsem, src)
            push(buf, ssem, rsem, src, False, has_left)

    def drain(buf, ssem, rsem, source=None):
        hop(buf, ssem, rsem, me, 2, across, source).wait_send()
        pl.when(has_right)(lambda: hop(buf, ssem, rsem, me, 0, me + 2, source).wait_send())
        pl.when(has_left)(lambda: hop(buf, ssem, rsem, me, 1, me - 2, source).wait_send())

        @pl.loop(1, length)
        def _(dist):
            @pl.when(a - dist >= 0)
            def _():
                src = me - 2 * dist
                hop(buf, ssem, rsem, src, 2, across).wait_send()
                pl.when(has_right)(lambda: hop(buf, ssem, rsem, src, 0, me + 2).wait_send())

            @pl.when(a + dist <= length - 1)
            def _():
                src = me + 2 * dist
                hop(buf, ssem, rsem, src, 2, across).wait_send()
                pl.when(has_left)(lambda: hop(buf, ssem, rsem, src, 1, me - 2).wait_send())

    push(slots, send, recv, me, has_right, has_left, f_ref)

    near = jnp.minimum(a, length - 1 - a)

    def place(k):
        dist = jnp.where(k <= 2 * near, (k + 1) // 2, k - near)
        left = jnp.where(k <= 2 * near, k % 2 == 1, a >= length - 1 - a)
        return jnp.where(left, a - dist, a + dist)

    def normalize(load):
        step = 32

        @pl.loop(0, tok // step, unroll=2)
        def _(i):
            at = pl.ds(pl.multiple_of(i * step, step), step)
            x = load(at).astype(F32)
            mean = jnp.mean(x, axis=-1, keepdims=True)
            c = x - mean
            var = jnp.mean(c * c, axis=-1, keepdims=True)
            nrm[at, :] = (c * lax.rsqrt(var + 1e-05) * gain_ref[...]).astype(BF16)

    def attend():
        tile = 256
        for c in range(d // tile):
            kb[:, c * tile : (c + 1) * tile] = jnp.dot(
                nrm[...], w[:, d + c * tile : d + (c + 1) * tile], preferred_element_type=F32
            ).astype(BF16)
        for c in range(d // tile):
            vt[c * tile : (c + 1) * tile, :] = lax.dot_general(
                wvt[c * tile : (c + 1) * tile, :], nrm[...], NT, preferred_element_type=F32
            ).astype(BF16)

        @pl.loop(0, HEADS // GROUP)
        def _(g):
            for j in range(GROUP):
                h = g * GROUP + j
                cols = pl.ds(pl.multiple_of((g * GROUP + j // 2 * 2) * hd, 2 * hd), 2 * hd)
                at = pl.ds(pl.multiple_of(h * hd, hd), hd)
                s = jnp.dot(kb[:, cols], qt[h], preferred_element_type=F32)
                old = top[h]
                new = jnp.maximum(old, jnp.max(s, axis=0, keepdims=True))
                fade = jnp.exp(old - new)
                p = jnp.exp(s - new)
                top[h] = new
                total[h] = total[h] * fade + jnp.sum(p, axis=0, keepdims=True)
                acc[at, :] = acc[at, :] * fade + jnp.dot(
                    vt[at, :], p.astype(BF16), preferred_element_type=F32
                )

    normalize(lambda at: f_ref[at, :])
    copies[0].wait()
    pair = 2 * hd
    upper = lax.broadcasted_iota(jnp.int32, (pair, tok), 0) < hd
    for c in range(HEADS // 2):
        q = jnp.dot(nrm[...], w[:, c * pair : (c + 1) * pair], preferred_element_type=F32)
        q = jnp.transpose(q * (1.0 / hd**0.5))
        qt[2 * c] = jnp.where(upper, q, 0.0).astype(BF16)
        qt[2 * c + 1] = jnp.where(upper, 0.0, q).astype(BF16)
    for c in range(d // 128):
        part = w[:, 2 * d + c * 128 : 2 * d + (c + 1) * 128].astype(F32)
        wvt[c * 128 : (c + 1) * 128, :] = jnp.transpose(part).astype(BF16)
    top[...] = jnp.full(top.shape, -1e30, F32)
    total[...] = jnp.zeros_like(total)
    acc[...] = jnp.zeros_like(acc)

    @pl.loop(0, n)
    def _(t):
        odd = t % 2 == 1
        by_line = jnp.logical_and(odd, t < n - 1)

        @pl.when(by_line)
        def _():
            relay(slots, send, recv, (t + 1) // 2)

        near_k = jnp.where(by_line, (t + 1) // 2, jnp.where(odd, length - 1, t // 2 - 1))
        src = jnp.where(
            t == 0, me, place(jnp.maximum(near_k, 0)) * 2 + jnp.where(by_line, b, 1 - b)
        )

        @pl.when(jnp.logical_and(t > 0, jnp.logical_not(by_line)))
        def _():
            landed(slots, send, recv, src)

        @pl.when(t > 0)
        def _():
            normalize(lambda at: slots[src, at, :])

        attend()

    tile = 256
    per = tile // hd
    for c in range(d // tile):
        o = jnp.concatenate(
            [
                acc[h * hd : (h + 1) * hd, :] / total[h]
                for h in range(c * per, (c + 1) * per)
            ],
            axis=0,
        )
        nrm[:, c * tile : (c + 1) * tile] = jnp.transpose(o).astype(BF16)
    copies[1].wait()
    for c in range(d // tile):
        cols = slice(c * tile, (c + 1) * tile)
        mixed_ref[:, cols] = (
            f_ref[:, cols].astype(F32)
            + jnp.dot(nrm[...], wo[:, cols], preferred_element_type=F32)
        ).astype(BF16)

    q = index_ref.shape[1]
    at = lax.broadcasted_iota(jnp.int32, (tok, q), 0)
    slot = lax.broadcasted_iota(jnp.int32, (tok, q), 1)
    chosen = jnp.logical_and(at == index_ref[...], slot < counts_ref[me])
    chosen = jnp.transpose(jnp.where(chosen, 1.0, 0.0).astype(F32)).astype(BF16)
    rows[me] = jnp.dot(chosen, mixed_ref[...], preferred_element_type=F32).astype(BF16)
    push(rows, rsend, rrecv, me, has_right, has_left)

    @pl.loop(1, length)
    def _(dist):
        relay(rows, rsend, rrecv, dist)

    @pl.loop(0, length)
    def _(k):
        landed(rows, rsend, rrecv, place(k) * 2 + 1 - b)

    scale = 1.0 / d**0.5
    for f0 in range(0, n, 8):
        fn = min(8, n - f0)
        block = rows[f0 : f0 + fn].reshape(fn * q, d)
        got = lax.dot_general(block, mixed_ref[...], NT, preferred_element_type=F32)
        for f in range(fn):
            factor = jnp.where(owner_ref[f0 + f] == me, scale, 0.0).astype(F32)
            corr_ref[0, f0 + f] = got[f * q : (f + 1) * q, :] * factor

    drain(slots, send, recv, f_ref)
    drain(rows, rsend, rrecv)


def solution(mesh):
    n = mesh.shape["frame"]

    def per_device(features, norm_gain, w_qkv, w_out, counts, query_index, owner):
        tok, d = features.shape
        q = query_index.shape[1]
        hd = d // HEADS
        vmem = pl.BlockSpec(memory_space=pltpu.VMEM)
        smem = pl.BlockSpec(memory_space=pltpu.SMEM)
        hbm = pl.BlockSpec(memory_space=pl.ANY)
        dma = pltpu.SemaphoreType.DMA
        return pl.pallas_call(
            functools.partial(kernel, n),
            out_shape=(
                jax.ShapeDtypeStruct((tok, d), BF16),
                jax.ShapeDtypeStruct((1, n, q, tok), F32),
            ),
            in_specs=[vmem, vmem, hbm, hbm, smem, vmem, smem],
            out_specs=(vmem, vmem),
            scratch_shapes=[
                pltpu.VMEM((n, tok, d), BF16),
                pltpu.VMEM((d, 3 * d), BF16),
                pltpu.VMEM((d, d), BF16),
                pltpu.VMEM((d, d), BF16),
                pltpu.VMEM((tok, d), BF16),
                pltpu.VMEM((HEADS, 2 * hd, tok), BF16),
                pltpu.VMEM((tok, d), BF16),
                pltpu.VMEM((d, tok), BF16),
                pltpu.VMEM((d, tok), F32),
                pltpu.VMEM((HEADS, 1, tok), F32),
                pltpu.VMEM((HEADS, 1, tok), F32),
                pltpu.VMEM((n, q, d), BF16),
                dma((2,)),
                dma((n // 2, 3)),
                dma((n,)),
                dma((n // 2, 3)),
                dma((n,)),
            ],
            compiler_params=pltpu.CompilerParams(
                collective_id=0, has_side_effects=True, vmem_limit_bytes=60 * 1024 * 1024
            ),
        )(features, norm_gain.reshape(1, d), w_qkv, w_out, counts, query_index, owner)

    in_specs = (
        P(("scene", "frame"), None),
        P(),
        P(),
        P(),
        P("scene"),
        P(("scene", "frame"), None),
        P("scene"),
    )
    out_specs = (P(("scene", "frame"), None), P(("scene", "frame"), None, None, None))
    return jax.shard_map(
        per_device, mesh=mesh, in_specs=in_specs, out_specs=out_specs, check_vma=False
    )
```

time: 232 us -> 87.1 us (0.38)
  waiting for transfers between devices: 110 us -> 0 us
  Pallas kernels: 0 us -> 82.7 us
  matrix products: 40.9 us -> 0 us
  blocking collectives: 31.6 us -> 0 us
  other arithmetic: 18.7 us -> 0 us
  between operations: 14.2 us -> 0.64 us
  local copies, waits for them, and re-layouts: 15.5 us -> 3.54 us
    all_gather x2 -> x0, waiting for transfers between devices: 109 us -> none  [the longest x1 72.1 us: per_device(): kpart = lax.all_gather(keys, 'frame', axis=0, tiled=True)]
    pallas_call x0 -> x1, Pallas kernels: none -> 82.7 us  [per_device(): pl.pallas_call(functools.partial(kernel, n), out_shape=(jax.ShapeDtypeStr...]
    dot_general x5 -> x0, matrix products: 40.9 us -> none  [the longest x1 15.8 us: per_device(): jnp.einsum('thd,shd->hts', queries, kpart.reshape(count, HEADS, head_dim)...]
    all_gather x1 -> x0, blocking collectives: 31.6 us -> none  [per_device(): arrived = lax.all_gather(picked[None], 'frame', axis=0, tiled=True)]
    reduce_sum x3 -> x0, other arithmetic: 16.6 us -> none  [the longest x1 14 us: per_device(): total = jnp.sum(weights, axis=-1)]
    all_gather x2 -> x0, local copies, waits for them, and re-layouts: 13 us -> none  [the longest x1 6.5 us: per_device(): kpart = lax.all_gather(keys, 'frame', axis=0, tiled=True)]
    unnamed x12 -> x2, local copies, waits for them, and re-layouts: 0.03 us -> 3.54 us
  transfers between devices with their start and end apart: 2 -> 0, of which waited for: 2 -> 0; matrix products, arithmetic and copies ran while one was open for 17% -> 0% of each run, Pallas kernels for 0% -> 0%
where the time goes in v1:
time: 87.1 us; the launch traced here: 86.9 us
  Pallas kernels  82.7 us (95%)
  local copies, waits for them, and re-layouts  3.54 us (4%)
    pallas_call x1, Pallas kernels, per_device(): pl.pallas_call(functools.partial(kernel, n), out_shape=(jax.ShapeDtypeStr...  82.7 us
    unnamed x2, local copies, waits for them, and re-layouts  3.54 us

profile of v1, /device:TPU:0, one launch (start us, length us, event | category | flops | bytes accessed | tf_op | source)
XLA Modules:
  0.0 86.9 jit_solution(9946278120597625723)
XLA Ops:
  0.6 82.7 %shard_map.86 = (bf16[256,1024]{1,0:T(8,128)(2,1)}, f32[1,8,32,256]{3,2,1,0:T(8,128)}) custom-call(bf16[256,1024]{1,0:T(8,128)(2,1)} %f_ref.1, f32[1,1024]{1,0:T(1,128)} %bitcast.1, bf16[1024,3072]{1,0:T(8,128)(2,1)} %wqkv_hbm.1, bf16[1024,1024]{1,0:T(8,128)(2,1)} %wo_hbm.1, s32[8]{0:T(128)} %counts_ref.1, s32[1,32]{1,0:T(1,128)} %index_ref.1, s32[8]{0:T(128)} %owner_ref.1), custom_call_target="tpu_custom_call" | custom-call | tf_op jit(solution)/shard_map/pallas_call | solution.py:250
  83.4 1.9 %copy.11 = bf16[256,1024]{1,0:T(8,128)(2,1)} copy(bf16[256,1024]{1,0:T(8,128)(2,1)} %get-tuple-element.4) | data formatting | bytes 1048576
  85.3 1.7 %copy.12 = f32[1,8,32,256]{3,2,1,0:T(8,128)} copy(f32[1,8,32,256]{3,2,1,0:T(8,128)} %get-tuple-element.5) | data formatting | bytes 524288

commit v2 on v1

--- a/solution.py
+++ b/solution.py
@@ -12,7 +12,7 @@
 F32 = jnp.float32
 BF16 = jnp.bfloat16
 NT = (((1,), (1,)), ((), ()))
-GROUP = 4
+GROUP = 8
 
 
 def kernel(
@@ -133,19 +133,25 @@
 
         @pl.loop(0, HEADS // GROUP)
         def _(g):
+            hs = [g * GROUP + j for j in range(GROUP)]
+            ss, ps, fades = [], [], []
             for j in range(GROUP):
-                h = g * GROUP + j
                 cols = pl.ds(pl.multiple_of((g * GROUP + j // 2 * 2) * hd, 2 * hd), 2 * hd)
-                at = pl.ds(pl.multiple_of(h * hd, hd), hd)
-                s = jnp.dot(kb[:, cols], qt[h], preferred_element_type=F32)
+                ss.append(jnp.dot(kb[:, cols], qt[hs[j]], preferred_element_type=F32))
+            for j in range(GROUP):
+                h, s = hs[j], ss[j]
                 old = top[h]
                 new = jnp.maximum(old, jnp.max(s, axis=0, keepdims=True))
                 fade = jnp.exp(old - new)
                 p = jnp.exp(s - new)
                 top[h] = new
                 total[h] = total[h] * fade + jnp.sum(p, axis=0, keepdims=True)
-                acc[at, :] = acc[at, :] * fade + jnp.dot(
-                    vt[at, :], p.astype(BF16), preferred_element_type=F32
+                fades.append(fade)
+                ps.append(p.astype(BF16))
+            for j in range(GROUP):
+                at = pl.ds(pl.multiple_of(hs[j] * hd, hd), hd)
+                acc[at, :] = acc[at, :] * fades[j] + jnp.dot(
+                    vt[at, :], ps[j], preferred_element_type=F32
                 )
 
     normalize(lambda at: f_ref[at, :])

time: 87.1 us -> 77.1 us (0.89)
  Pallas kernels: 82.7 us -> 72.7 us
    pallas_call x1, Pallas kernels: 82.7 us -> 72.7 us  [per_device(): pl.pallas_call(functools.partial(kernel, n), out_shape=(jax.ShapeDtypeStr...]
where the time goes in v2:
time: 77.1 us; the launch traced here: 76.9 us
  Pallas kernels  72.7 us (94%)
  local copies, waits for them, and re-layouts  3.54 us (5%)
    pallas_call x1, Pallas kernels, per_device(): pl.pallas_call(functools.partial(kernel, n), out_shape=(jax.ShapeDtypeStr...  72.7 us
    unnamed x2, local copies, waits for them, and re-layouts  3.54 us

profile of v2, /device:TPU:0, one launch (start us, length us, event | category | flops | bytes accessed | tf_op | source)
XLA Modules:
  0.0 76.9 jit_solution(719413184818614336)
XLA Ops:
  0.6 72.7 %shard_map.86 = (bf16[256,1024]{1,0:T(8,128)(2,1)}, f32[1,8,32,256]{3,2,1,0:T(8,128)}) custom-call(bf16[256,1024]{1,0:T(8,128)(2,1)} %f_ref.1, f32[1,1024]{1,0:T(1,128)} %bitcast.1, bf16[1024,3072]{1,0:T(8,128)(2,1)} %wqkv_hbm.1, bf16[1024,1024]{1,0:T(8,128)(2,1)} %wo_hbm.1, s32[8]{0:T(128)} %counts_ref.1, s32[1,32]{1,0:T(1,128)} %index_ref.1, s32[8]{0:T(128)} %owner_ref.1), custom_call_target="tpu_custom_call" | custom-call | tf_op jit(solution)/shard_map/pallas_call | solution.py:256
  73.3 1.9 %copy.11 = bf16[256,1024]{1,0:T(8,128)(2,1)} copy(bf16[256,1024]{1,0:T(8,128)(2,1)} %get-tuple-element.4) | data formatting | bytes 1048576
  75.2 1.7 %copy.12 = f32[1,8,32,256]{3,2,1,0:T(8,128)} copy(f32[1,8,32,256]{3,2,1,0:T(8,128)} %get-tuple-element.5) | data formatting | bytes 524288
